TPU v7x, 32 devices: a whole 2x2x4 slice. The times are simulated.
32 devices in a mesh: front: 4 (over z), row: 4 (over x, core), col: 2 (over y).
Axes of the slice: x: 2, y: 2, z: 4, core: 2. Of those that a mesh axis runs over, the one named last changes fastest.
Arguments:
- front_slab: bfloat16 [4, 2048, 8192], P('front', 'row', 'col'), may hold values from -0.0625 to 0.0625
- samples: bfloat16 [8192, 256], P(('row', 'col')), may hold values from -6 to 6
- child_tiles: bfloat16 [64, 128, 2048], P(('front', 'row', 'col')), may hold values from -0.125 to 0.125
- parent_front: int32 [64, 1], P(('front', 'row', 'col')), may hold values from 0 to 3; in each aligned block of 2 rows (0 to 1, 2 to 3, ...) at most 2 rows name the same one
- parent_tile: int32 [64], P(('front', 'row', 'col')), may hold values from 0 to 15
- column_tiles: int32 [64, 16], P(('front', 'row', 'col')), may hold values from 0 to 63
- ranks: int32 [4, 4], P('front', 'row'), may hold values from 128 to 256
Outputs:
- sampled: float32 [4, 2048, 256], P('front', ('row', 'col'))
- bases: float32 [4, 2048, 256], P('front', ('row', 'col'))
Inputs may be any that keep to these rules, and one draw needn't show every extreme that they name: `parent_front`: among the 2 tiles of one device, at most 2 name the same parent front.
All inputs are finite; a program needn't handle non-finite values.
Results may differ from a plain program's by a relative error of at most 0.0003.
Values may be sent and summed in bfloat16 or wider, within the bound.
A program may use at most 64 MiB of HBM per device.

v0:
```python
import jax
import jax.numpy as jnp
from jax import lax
from jax.sharding import PartitionSpec as P


def on_device(front_slab, samples, child_tiles, parent_front, parent_tile, column_tiles, ranks):
    width = samples.shape[1]
    slab = front_slab[0]
    col_width = slab.shape[1]
    omega = lax.all_gather(samples, ("row", "col"), axis=0, tiled=True)
    full = omega.shape[0]
    own = lax.dynamic_slice_in_dim(omega, lax.axis_index("col") * col_width, col_width, 0)
    direct = lax.psum_scatter(
        jnp.dot(slab, own, preferred_element_type=jnp.float32),
        "col",
        scatter_dimension=0,
        tiled=True,
    )
    tile_count = child_tiles.shape[0]
    blocks = child_tiles.shape[2] // 128
    omega_tiles = omega.reshape(full // 128, 128, width)
    chosen = omega_tiles[column_tiles]
    pieces = child_tiles.reshape(tile_count, 128, blocks, 128)
    product = jnp.einsum("trkc,tkcs->trs", pieces, chosen, preferred_element_type=jnp.float32)
    parents = lax.axis_size("front")
    row_tiles = slab.shape[0] * lax.axis_size("row") // 128
    dest = parent_front[:, 0]
    capacity = max(2, 2 * ((tile_count + parents - 1) // parents))
    match = (dest[:, None] == jnp.arange(parents, dtype=jnp.int32)[None, :]).astype(jnp.int32)
    before = jnp.cumsum(match, axis=0) - match
    slot = dest * capacity + jnp.sum(before * match, axis=1)
    place = (slot[:, None] == jnp.arange(parents * capacity, dtype=jnp.int32)[None, :]).astype(
        jnp.float32
    )
    sent = jnp.einsum("tq,trs->qrs", place, product, precision=lax.Precision.HIGHEST)
    sent = sent.reshape(parents, capacity, 128, width)
    labels = (
        jnp.dot(parent_tile.astype(jnp.float32) + 1.0, place, precision=lax.Precision.HIGHEST) - 1.0
    )
    labels = labels.reshape(parents, capacity)
    arrived, arrived_labels = (
        lax.all_to_all(sent, "front", split_axis=0, concat_axis=0, tiled=True),
        lax.all_to_all(labels, "front", split_axis=0, concat_axis=0, tiled=True),
    )
    tile_index = arrived_labels.reshape(-1).astype(jnp.int32)
    spread = (tile_index[:, None] == jnp.arange(row_tiles, dtype=jnp.int32)[None, :]).astype(
        jnp.float32
    )
    gathered = arrived.reshape(parents * capacity, 128, width)
    rows_full = jnp.einsum("qj,qrs->jrs", spread, gathered, precision=lax.Precision.HIGHEST)
    rows_full = rows_full.reshape(row_tiles * 128, width)
    extended = lax.psum_scatter(rows_full, ("row", "col"), scatter_dimension=0, tiled=True)
    sampled = direct + extended
    mask = (jnp.arange(width, dtype=jnp.int32) < ranks[0, 0]).astype(jnp.float32)
    masked = sampled * mask[None, :]
    partial_gram = jnp.dot(masked.T, masked, precision=lax.Precision.HIGHEST)
    gram = lax.psum(partial_gram, "col") + jnp.diag(1.0 - mask)
    lower = jnp.linalg.cholesky(gram)
    basis = lax.linalg.triangular_solve(
        lower, masked, left_side=False, lower=True, transpose_a=True
    )
    return (sampled[None], basis[None])


def solution(mesh):
    in_specs = (
        P("front", "row", "col"),
        P(("row", "col"), None),
        P(("front", "row", "col"), None, None),
        P(("front", "row", "col"), None),
        P(("front", "row", "col")),
        P(("front", "row", "col"), None),
        P("front", "row"),
    )
    out_specs = (P("front", ("row", "col"), None), P("front", ("row", "col"), None))
    return jax.shard_map(
        on_device, mesh=mesh, in_specs=in_specs, out_specs=out_specs, check_vma=False
    )
```

profile of v0, /device:TPU:0, one launch (start us, length us, event | category | flops | bytes accessed | tf_op | source)
XLA Modules:
  0.0 227.8 jit_solution(5286594842311993352)
XLA Ops:
  7.9 0.7 fusion.25
  8.7 0.8 select_reduce_fusion.2
  10.2 0.8 fusion.8
  11.7 6.3 %all-to-all-start = ((f32[4,1,2]{2,1,0:T(1,128)}), f32[4,1,2]{2,1,0:T(1,128)S(1)}, u32[]{:S(2)}, u32[]{:S(2)}) async-start(f32[4,1,2]{2,1,0:T(1,128)} %bitcast.7), calls=%async_computation.1 | async-start | bytes 4096 | tf_op jit(solution)/shard_map/all_to_all | solution.py:44
  18.0 0.7 compare_select_fusion
  18.8 30.4 %all-gather.2.cloned.1.call-done = bf16[8192,256]{1,0:T(8,128)(2,1)} async-done(((bf16[1024,256]{1,0:T(8,128)(2,1)}), bf16[8192,256]{1,0:T(8,128)(2,1)}) %all-gather.2.cloned.1.call-update) | async-done | bytes 4194320 | tf_op jit(solution)/shard_map/all_gather | solution.py:11
  49.2 2.9 %gather_fusion = bf16[32,128,256]{2,1,0:T(8,128)(2,1)S(1)} fusion(bf16[64,128,256]{2,1,0:T(8,128)(2,1)} %bitcast.97, s32[1024]{0:T(1024)S(1)} %pad_clamp_fusion), kind=kCustom, calls=%fused_computation | custom fusion | bytes 4194432 | tf_op jit(solution)/shard_map/gather | solution.py:23
  52.1 1.0 convolution_bitcast_fusion
  53.2 0.8 fusion.23
  54.6 1.3 copy.47
  56.0 4.6 %all-to-all-start.1 = ((f32[4,2,128,256]{3,1,2,0:T(2,128)}), f32[4,2,128,256]{3,1,2,0:T(2,128)S(1)}, u32[]{:S(2)}, u32[]{:S(2)}) async-start(f32[4,2,128,256]{3,1,2,0:T(2,128)} %copy.47), calls=%async_computation.2 | async-start | bytes 2097152 | tf_op jit(solution)/shard_map/all_to_all | solution.py:43
  60.6 4.9 %fusion.3 = f32[512,256]{0,1:T(8,128)} fusion(bf16[1,512,4096]{2,1,0:T(8,128)(2,1)} %param.7, bf16[8192,256]{1,0:T(8,128)(2,1)} %all-gather.2.cloned.1.call-done, s32[]{:T(128)S(6)} %select_n.15), kind=kOutput, calls=%fused_computation.7 | convolution fusion | flops 1073741824 | bytes 6815748 | tf_op jit(solution)/shard_map/dot_general | solution.py:15
  65.7 21.0 %all-to-all-done.1 = f32[4,2,128,256]{3,1,2,0:T(2,128)S(1)} async-done(((f32[4,2,128,256]{3,1,2,0:T(2,128)}), f32[4,2,128,256]{3,1,2,0:T(2,128)S(1)}, u32[]{:S(2)}, u32[]{:S(2)}) %all-to-all-start.1) | async-done | bytes 1048608 | tf_op jit(solution)/shard_map/all_to_all | solution.py:43
  86.7 1.2 copy.64
  87.9 1.1 fusion.20
  89.0 2.2 copy.74
  92.2 38.5 %reduce-scatter.5.cloned.1.call-done = f32[256,256]{0,1:T(8,128)} async-done(((f32[2048,256]{0,1:T(8,128)}), f32[256,256]{0,1:T(8,128)}) %reduce-scatter.5.cloned.1.call-update) | async-done | bytes 262160 | tf_op jit(solution)/shard_map/reduce_scatter | solution.py:53
  130.7 1.1 broadcast_multiply_fusion
  131.8 1.1 fusion.34
  133.0 0.8 copy.57
  133.8 22.9 %all-reduce.3.cloned.1.call-done = f32[256,256]{0,1:T(8,128)} async-done(((f32[256,256]{0,1:T(8,128)}), f32[256,256]{0,1:T(8,128)}) %all-reduce.3.cloned.1.call-update) | async-done | bytes 262160 | tf_op jit(solution)/shard_map/psum | solution.py:58
  156.7 1.0 select_add_fusion
  157.8 1.0 fusion.11
  158.9 11.7 %cholesky.49 = f32[128,128]{1,0:T(8,128)S(1)} custom-call(f32[128,128]{1,0:T(8,128)S(1)} %cholesky.115), custom_call_target="Cholesky" | custom-call | tf_op jit(solution)/shard_map/jit(cholesky)/cholesky | solution.py:59
  170.7 9.8 %custom-call.14 = f32[1,128,128]{1,2,0:T(8,128)S(1)} custom-call(f32[1,128,128]{2,1,0:T(8,128)S(1)} %get-tuple-element.47), custom_call_target="InvertDiagBlocksLowerTriangular" | custom-call | tf_op jit(solution)/shard_map/jit(cholesky)/cholesky | solution.py:59
  181.1 11.7 %cholesky.103 = f32[128,128]{1,0:T(8,128)S(1)} custom-call(f32[128,128]{1,0:T(8,128)S(1)} %convolution_subtract_fusion.1), custom_call_target="Cholesky" | custom-call | tf_op jit(solution)/shard_map/jit(cholesky)/cholesky | solution.py:59
  193.0 0.7 compare_reduce_fusion
  195.2 4.5 %while.1 = (s32[]{:T(128)}, f32[256,256]{0,1:T(8,128)S(1)}, s32[2,2]{1,0:T(2,128)S(1)}, f32[2,128,128]{2,1,0:T(8,128)S(1)}, s32[]{:T(128)}) while((s32[]{:T(128)}, f32[256,256]{0,1:T(8,128)S(1)}, s32[2,2]{1,0:T(2,128)S(1)}, f32[2,128,128]{2,1,0:T(8,128)S(1)}, s32[]{:T(128)}) %tuple.34), condition=%wide.while_cond, body=%wide.while_body.sunk | while | flops 2 | bytes 393329 | solution.py:60
  196.0 1.4 dynamic-slice.7
  198.1 1.4 dynamic-slice.7
  199.7 19.7 %custom-call.15 = f32[2,128,128]{1,2,0:T(8,128)S(1)} custom-call(f32[2,128,128]{2,1,0:T(8,128)S(1)} %get-tuple-element.9), custom_call_target="InvertDiagBlocksLowerTriangular" | custom-call | tf_op jit(solution)/shard_map/triangular_solve | solution.py:60
  220.4 0.8 copy.58
  (51 shorter events, 6.9 us)
Async XLA Ops:
  7.2 44.9 %copy-start = (bf16[2,128,2048]{2,1,0:T(8,128)(2,1)S(1)}, bf16[2,128,2048]{2,1,0:T(8,128)(2,1)}, u32[]{:S(2)}) copy-start(bf16[2,128,2048]{2,1,0:T(8,128)(2,1)} %param.9) | copy-start | bytes 3145732
  7.2 42.0 %all-gather.2.cloned.1.call-start = ((), (), s32[]{:S(2)}) async-start(), calls=%async_computation.4 | async-start | bytes 4718592 | tf_op jit(solution)/shard_map/all_gather | solution.py:11
  11.7 44.3 %all-to-all-start = ((f32[4,1,2]{2,1,0:T(1,128)}), f32[4,1,2]{2,1,0:T(1,128)S(1)}, u32[]{:S(2)}, u32[]{:S(2)}) async-start(f32[4,1,2]{2,1,0:T(1,128)} %bitcast.7), calls=%async_computation.1 | async-start | bytes 4096 | tf_op jit(solution)/shard_map/all_to_all | solution.py:44
  56.0 30.7 %all-to-all-start.1 = ((f32[4,2,128,256]{3,1,2,0:T(2,128)}), f32[4,2,128,256]{3,1,2,0:T(2,128)S(1)}, u32[]{:S(2)}, u32[]{:S(2)}) async-start(f32[4,2,128,256]{3,1,2,0:T(2,128)} %copy.47), calls=%async_computation.2 | async-start | bytes 2097152 | tf_op jit(solution)/shard_map/all_to_all | solution.py:43
  60.6 31.6 %reduce-scatter.3.cloned.1.call-start = ((), (), s32[]{:S(2)}) async-start(), calls=%async_computation.5 | async-start | bytes 786432 | tf_op jit(solution)/shard_map/reduce_scatter | solution.py:14
  65.5 65.2 %reduce-scatter.5.cloned.1.call-start = ((), (), s32[]{:S(2)}) async-start(), calls=%async_computation.6 | async-start | bytes 2359296 | tf_op jit(solution)/shard_map/reduce_scatter | solution.py:53
  91.3 65.4 %all-reduce.3.cloned.1.call-start = ((), (), s32[]{:S(2)}) async-start(), calls=%async_computation.7 | async-start | bytes 524288 | tf_op jit(solution)/shard_map/psum | solution.py:58
Sparse Core Ops, SparseCore 0:
  9.9 39.2 all-gather.1
  65.6 15.1 reduce-scatter.2
  91.4 39.2 reduce-scatter.4
  133.4 23.2 all-reduce.2
where the time goes:
time: 228 us
  waiting for transfers between devices  114 us (50%)
  other arithmetic  59.9 us (26%)
  between operations  16 us (7%)
  local copies, waits for them, and re-layouts  15.7 us (7%)
  starting transfers between devices  11.3 us (5%)
  matrix products  11.2 us (5%)
    reduce_scatter x1, waiting for transfers between devices, on_device(): lax.psum_scatter(rows_full, ('row', 'col'), scatter_dimension=0, tiled=True)  38.5 us
    another operation x6, other arithmetic, on_device(): lower = jnp.linalg.cholesky(gram)  34 us
    all_gather x1, waiting for transfers between devices, on_device(): omega = lax.all_gather(samples, ('row', 'col'), axis=0, tiled=True)  30.4 us
    psum x1, waiting for transfers between devices, on_device(): gram = lax.psum(partial_gram, 'col') + jnp.diag(1.0 - mask)  22.9 us
    all_to_all x1, waiting for transfers between devices, on_device(): lax.all_to_all(sent, 'front', split_axis=0, concat_axis=0, tiled=True)  21 us
    another operation x3, other arithmetic, on_device(): lax.linalg.triangular_solve(lower, masked, left_side=False, lower=True, t...  19.7 us
    all_to_all x1, starting transfers between devices, on_device(): lax.all_to_all(labels, 'front', split_axis=0, concat_axis=0, tiled=True)  6.35 us
    dot_general x1, matrix products, on_device(): jnp.dot(slab, own, preferred_element_type=jnp.float32)  4.93 us
  transfers between devices with their start and end apart: 6, of which 4 were waited for; matrix products, arithmetic and copies ran while one was open for 9% of the time, Pallas kernels for 0%

commit v1 on v0

v1 whole, which is shorter than its diff:
```python
import functools

import jax
import jax.numpy as jnp
from jax import lax
from jax.experimental import pallas as pl
from jax.experimental.pallas import tpu as pltpu
from jax.sharding import PartitionSpec as P

F32 = jnp.float32
HI = lax.Precision.HIGHEST
LOGICAL = pl.DeviceIdType.MESH


def dot_nt(a, b):
    return lax.dot_general(a, b, (((1,), (1,)), ((), ())), precision=HI, preferred_element_type=F32)


def inverse_factor(a):
    n = a.shape[0]
    tiles = n // 8
    w = [a[8 * t : 8 * t + 8, :] for t in range(tiles)]
    lane = lax.broadcasted_iota(jnp.int32, (8, n), 1)
    sub = lax.broadcasted_iota(jnp.int32, (8, n), 0)
    rows = []
    for t in range(tiles):
        base = 8 * t
        inside = (lane >= base) & (lane < base + 8)
        cols = [jnp.broadcast_to(w[t][:, base + k : base + k + 1], (8, n)) for k in range(8)]
        v = jnp.where(inside, jnp.where(lane - base == sub, 1.0, 0.0), w[t])
        done, pivots = v, cols[0]
        for k in range(8):
            here = sub == k
            pivot = jnp.broadcast_to(cols[k][k : k + 1, :], (8, n))
            inv = 1.0 / pivot
            done = jnp.where(here, v, done)
            pivots = jnp.where(here, pivot, pivots)
            step = jnp.broadcast_to(v[k : k + 1, :], (8, n)) * inv
            v = jnp.where(here, step, v - cols[k] * step)
            for m in range(k + 1, 8):
                step = jnp.broadcast_to(cols[m][k : k + 1, :], (8, n)) * inv
                cols[m] = jnp.where(here, step, cols[m] - cols[k] * step)
        rows.append(jnp.where(lane < base + 8, done, 0.0) * lax.rsqrt(pivots))
        vk = [jnp.broadcast_to(v[k : k + 1, :], (8, n)) for k in range(8)]
        for u in range(t + 1, tiles):
            x = jnp.where(inside, 0.0, w[u])
            terms = [
                jnp.broadcast_to(w[u][:, base + k : base + k + 1], (8, n)) * vk[k] for k in range(8)
            ]
            low = (terms[0] + terms[1]) + (terms[2] + terms[3])
            high = (terms[4] + terms[5]) + (terms[6] + terms[7])
            w[u] = x - (low + high)
    return jnp.concatenate(rows, axis=0)


def basis_kernel(rank_ref, sampled_ref, gram_ref, out_ref, basis_ref):
    half = gram_ref.shape[1]
    rank = rank_ref[0, 0]
    sampled = sampled_ref[...]
    out_ref[...] = sampled
    rows = sampled.shape[0]
    lane = lax.broadcasted_iota(jnp.int32, (rows, half), 1)
    first = jnp.where(lane < rank, sampled[:, :half], 0.0)
    second = jnp.where(lane + half < rank, sampled[:, half:], 0.0)
    r = lax.broadcasted_iota(jnp.int32, (half, half), 0)
    c = lax.broadcasted_iota(jnp.int32, (half, half), 1)
    a = gram_ref[0] + jnp.where((r == c) & (c >= rank), 1.0, 0.0)
    inv1 = inverse_factor(a)
    low = dot_nt(gram_ref[1], inv1)
    a = gram_ref[2] + jnp.where((r == c) & (c + half >= rank), 1.0, 0.0) - dot_nt(low, low)
    inv2 = inverse_factor(a)
    basis = dot_nt(first, inv1)
    basis_ref[:, :half] = basis
    basis_ref[:, half:] = dot_nt(second - dot_nt(basis, low), inv2)


def leaf_bases(sampled, gram, ranks):
    vmem = pl.BlockSpec(memory_space=pltpu.VMEM)
    return pl.pallas_call(
        basis_kernel,
        out_shape=(jax.ShapeDtypeStruct(sampled.shape, F32),) * 2,
        in_specs=[pl.BlockSpec(memory_space=pltpu.SMEM), vmem, vmem],
        out_specs=(vmem, vmem),
        name="leaf_bases",
    )(ranks, sampled, gram)


def sample_kernel(
    fronts,
    tile_ref,
    front_ref,
    column_ref,
    rank_ref,
    slab_ref,
    samples_ref,
    child_ref,
    sampled_ref,
    gram_ref,
    omega,
    slab,
    child,
    held,
    part,
    blocks,
    got1,
    got2,
    gram_own,
    gram_got,
    copy_sem,
    gs,
    gr,
    zs_right,
    zs_left,
    zs_pair,
    zr,
    zr_pair,
    es,
    er,
):
    f, r, c = lax.axis_index("front"), lax.axis_index("row"), lax.axis_index("col")
    x, core = r // 2, r % 2
    width = samples_ref.shape[2]
    half = width // 2
    chunk = samples_ref.shape[0]
    hc = chunk // 2
    count = child_ref.shape[0]
    slab_rows, slab_cols = slab_ref.shape
    own_rows = slab_rows // 2
    pieces = own_rows // 128
    row_tiles = slab_rows * 4 // 128
    r_x = (1 - x) * 2 + core
    r_p = x * 2 + (1 - core)
    to_x, to_y, to_p = (f, r_x, c), (f, r, 1 - c), (f, r_p, c)
    right, left = (f + 1, r, c), (f - 1, r, c)

    loads = [
        pltpu.make_async_copy(child_ref, child, copy_sem.at[0]),
        pltpu.make_async_copy(slab_ref, slab, copy_sem.at[1]),
        pltpu.make_async_copy(
            samples_ref, omega.at[pl.ds((r * 2 + c) * chunk, chunk)], copy_sem.at[2]
        ),
    ]
    loads[2].start()
    loads[0].start()
    loads[1].start()

    barrier = pltpu.get_barrier_semaphore()
    for target in (to_x, to_y, to_p):
        pl.semaphore_signal(barrier, inc=1, device_id=target, device_id_type=LOGICAL)

    @pl.when(f < fronts - 1)
    def _():
        pl.semaphore_signal(barrier, inc=1, device_id=right, device_id_type=LOGICAL)

    @pl.when(f > 0)
    def _():
        pl.semaphore_signal(barrier, inc=1, device_id=left, device_id_type=LOGICAL)

    pl.semaphore_wait(barrier, 3 + jnp.minimum(f, 1) + jnp.minimum(fronts - 1 - f, 1))

    def rcopy(src, dst, send, recv, target):
        return pltpu.make_async_remote_copy(
            src_ref=src,
            dst_ref=dst,
            send_sem=send,
            recv_sem=recv,
            device_id=target,
            device_id_type=LOGICAL,
        )

    def where_is(row, col, h):
        return pl.ds((row * 2 + col) * chunk + h * hc, hc)

    sent = []

    def send(src, place, n, target):
        cp = rcopy(src, omega.at[place], gs.at[n], gr.at[n], target)
        cp.start()
        sent.append(cp)

    def arrived(place, n):
        rcopy(omega.at[place], omega.at[place], gs.at[n], gr.at[n], to_p).wait_recv()

    own = [samples_ref.at[pl.ds(h * hc, hc)] for h in range(2)]
    for h in (0, 1):
        send(own[h], where_is(r, c, h), h, to_x)
        send(own[1 - h], where_is(r, c, 1 - h), 2 + 1 - h, to_y)
        send(own[h], where_is(r, c, h), 6 + h, to_p)
    place = where_is(r_x, c, 0)
    arrived(place, 0)
    send(omega.at[place], place, 4, to_y)
    send(omega.at[place], place, 8, to_p)
    place = where_is(r, 1 - c, 1)
    arrived(place, 3)
    send(omega.at[place], place, 5, to_x)
    send(omega.at[place], place, 11, to_p)
    place = where_is(r_x, c, 1)
    arrived(place, 1)
    send(omega.at[place], place, 9, to_p)
    place = where_is(r, 1 - c, 0)
    arrived(place, 2)
    send(omega.at[place], place, 10, to_p)
    for h in (0, 1):
        place = where_is(r_x, 1 - c, h)
        arrived(place, 4 + h)
        send(omega.at[place], place, 12 + h, to_p)
    for h in (0, 1):
        arrived(where_is(r_p, c, h), 6 + h)
        arrived(where_is(r_x + r_p - r, c, h), 8 + h)
        arrived(where_is(r_p, 1 - c, h), 10 + h)
        arrived(where_is(r_x + r_p - r, 1 - c, h), 12 + h)
    loads[2].wait()
    loads[0].wait()

    group = 2
    for t in range(count):
        acc = jnp.zeros((128, width), F32)
        for b in range(0, column_ref.shape[1], group):
            chosen = jnp.concatenate(
                [
                    omega[column_ref[t, b + g]]
                    for g in range(group)
                ],
                axis=0,
            )
            acc = acc + jnp.dot(
                child[t, :, 128 * b : 128 * (b + group)], chosen, preferred_element_type=F32
            )
        held[0, f, 128 * t : 128 * (t + 1), :] = acc
        label = (front_ref[t, 0] * row_tiles + tile_ref[t]).astype(F32)
        at = 128 * count + 8 * t
        held[0, f, at : at + 8, :] = jnp.full((8, width), label, F32)

    def along(src, sem, target):
        return rcopy(held.at[0, src], held.at[0, src], sem.at[src], zr.at[src], target)

    def across(src):
        return rcopy(held.at[0, src], held.at[1, src], zs_pair.at[src], zr_pair.at[src], to_p)

    @pl.when(f < fronts - 1)
    def _():
        along(f, zs_right, right).start()

    @pl.when(f > 0)
    def _():
        along(f, zs_left, left).start()

    across(f).start()

    loads[1].wait()

    @pl.loop(0, slab_rows // 128)
    def _(i):
        rows = pl.ds(pl.multiple_of(i * 128, 128), 128)
        part[rows, :] = jnp.dot(
            slab[rows, :],
            omega[pl.ds(c * (slab_cols // 128), slab_cols // 128)].reshape(slab_cols, width),
            preferred_element_type=F32,
        )

    for d in range(1, fronts):

        @pl.when(f >= d)
        def _():
            along(f - d, zs_right, right).wait_recv()

            @pl.when(f < fronts - 1)
            def _():
                along(f - d, zs_right, right).start()

            across(f - d).start()

        @pl.when(f + d < fronts)
        def _():
            along(f + d, zs_left, left).wait_recv()

            @pl.when(f > 0)
            def _():
                along(f + d, zs_left, left).start()

            across(f + d).start()

    for s in range(fronts):
        across(s).wait_recv()

    def fill(h, spot, row, col, piece_of_part):
        lanes = slice(h * half, (h + 1) * half)
        first = f * row_tiles + (row * 2 + col) * pieces
        for i in range(pieces):
            wanted = (first + i).astype(F32)
            masks = []
            for side in range(2):
                for s in range(fronts):
                    for t in range(count):
                        at = 128 * count + 8 * t
                        masks.append((side, s, t, held[side, s, at : at + 8, :half] == wanted))

            @pl.loop(0, 4)
            def _(q):
                accs = [jnp.zeros((8, half), F32)] * 4
                if piece_of_part is not None:
                    accs = [
                        part[
                            pl.ds(
                                pl.multiple_of(
                                    piece_of_part * own_rows + i * 128 + q * 32 + 8 * e, 8
                                ),
                                8,
                            ),
                            lanes,
                        ]
                        for e in range(4)
                    ]
                for side, s, t, mask in masks:
                    for e in range(4):
                        rows = pl.ds(pl.multiple_of(128 * t + q * 32 + 8 * e, 8), 8)
                        accs[e] = accs[e] + jnp.where(mask, held[side, s, rows, lanes], 0.0)
                for e in range(4):
                    rows = pl.ds(pl.multiple_of(i * 128 + q * 32 + 8 * e, 8), 8)
                    blocks[h, spot, rows, :] = accs[e]

    two = pl.ds(2, 2)
    fill(0, 2, r_x, c, None)
    fill(0, 3, r_x, 1 - c, None)
    a1 = rcopy(blocks.at[0, two], got1.at[0], es.at[0], er.at[0], to_x)
    a1.start()
    fill(1, 2, r, 1 - c, 1 - c)
    fill(1, 3, r_x, 1 - c, None)
    b1 = rcopy(blocks.at[1, two], got1.at[1], es.at[1], er.at[1], to_y)
    b1.start()
    fill(0, 1, r, 1 - c, 1 - c)
    fill(1, 1, r_x, c, None)
    fill(0, 0, r, c, c)
    fill(1, 0, r, c, c)
    a1.wait_recv()
    blocks[0, 1] = blocks[0, 1] + got1[0, 1]
    a2 = rcopy(blocks.at[0, 1], got2.at[0], es.at[2], er.at[2], to_y)
    a2.start()
    b1.wait_recv()
    blocks[1, 1] = blocks[1, 1] + got1[1, 1]
    b2 = rcopy(blocks.at[1, 1], got2.at[1], es.at[3], er.at[3], to_x)
    b2.start()
    a2.wait_recv()
    b2.wait_recv()
    lane = lax.broadcasted_iota(jnp.int32, (own_rows, half), 1)
    masked = []
    for h in range(2):
        total = (blocks[h, 0] + got1[h, 0]) + got2[h]
        sampled_ref[:, h * half : (h + 1) * half] = total
        masked.append(jnp.where(lane + h * half < rank_ref[0, 0], total, 0.0))
    for n, (i, j) in enumerate(((0, 0), (1, 0), (1, 1))):
        gram_own[n] = lax.dot_general(
            masked[i],
            masked[j],
            (((0,), (0,)), ((), ())),
            precision=HI,
            preferred_element_type=F32,
        )
    g = rcopy(gram_own, gram_got, es.at[4], er.at[4], to_y)
    g.start()
    for cp in sent:
        cp.wait_send()
    for s in range(fronts):
        across(s).wait_send()

        @pl.when((f < fronts - 1) & (f >= s))
        def _():
            along(s, zs_right, right).wait_send()

        @pl.when((f > 0) & (f <= s))
        def _():
            along(s, zs_left, left).wait_send()

    for cp in (a1, b1, a2, b2):
        cp.wait_send()
    g.wait()
    gram_ref[...] = gram_own[...] + gram_got[...]


def sampled_and_gram(
    fronts, slab, samples, child_tiles, parent_front, parent_tile, column_tiles, ranks
):
    width = samples.shape[1]
    half = width // 2
    count = child_tiles.shape[0]
    rows = slab.shape[0] // 2
    smem = pl.BlockSpec(memory_space=pltpu.SMEM)
    hbm = pl.BlockSpec(memory_space=pl.ANY)
    vmem = pl.BlockSpec(memory_space=pltpu.VMEM)
    dma = lambda n: pltpu.SemaphoreType.DMA((n,))
    return pl.pallas_call(
        functools.partial(sample_kernel, fronts),
        out_shape=(
            jax.ShapeDtypeStruct((rows, width), F32),
            jax.ShapeDtypeStruct((3, half, half), F32),
        ),
        in_specs=[smem] * 4 + [hbm] * 3,
        out_specs=(vmem, vmem),
        scratch_shapes=[
            pltpu.VMEM((samples.shape[0] // 128 * 8, 128, width), samples.dtype),
            pltpu.VMEM(slab.shape, slab.dtype),
            pltpu.VMEM(child_tiles.shape, child_tiles.dtype),
            pltpu.VMEM((2, fronts, 136 * count, width), F32),
            pltpu.VMEM((slab.shape[0], width), F32),
            pltpu.VMEM((2, 4, rows, half), F32),
            pltpu.VMEM((2, 2, rows, half), F32),
            pltpu.VMEM((2, rows, half), F32),
            pltpu.VMEM((3, half, half), F32),
            pltpu.VMEM((3, half, half), F32),
            dma(3),
            dma(14),
            dma(14),
            dma(fronts),
            dma(fronts),
            dma(fronts),
            dma(fronts),
            dma(fronts),
            dma(5),
            dma(5),
        ],
        compiler_params=pltpu.CompilerParams(
            collective_id=0, has_side_effects=True, vmem_limit_bytes=48 * 1024 * 1024
        ),
        name="sampled_and_gram",
    )(
        parent_tile,
        parent_front,
        column_tiles,
        ranks,
        slab,
        samples.reshape(-1, 128, width),
        child_tiles,
    )


def sampled_and_gram_any(
    slab, samples, child_tiles, parent_front, parent_tile, column_tiles, ranks
):
    width = samples.shape[1]
    half = width // 2
    col_width = slab.shape[1]
    omega = lax.all_gather(samples, ("row", "col"), axis=0, tiled=True)
    own = lax.dynamic_slice_in_dim(omega, lax.axis_index("col") * col_width, col_width, 0)
    direct = lax.psum_scatter(
        jnp.dot(slab, own, preferred_element_type=F32), "col", scatter_dimension=0, tiled=True
    )
    count = child_tiles.shape[0]
    blocks = child_tiles.shape[2] // 128
    chosen = omega.reshape(-1, 128, width)[column_tiles]
    pieces = child_tiles.reshape(count, 128, blocks, 128)
    product = jnp.einsum("trkc,tkcs->trs", pieces, chosen, preferred_element_type=F32)
    row_tiles = slab.shape[0] * lax.axis_size("row") // 128
    label = (parent_front[:, 0] * row_tiles + parent_tile).astype(F32)
    product = lax.all_gather(product, "front", axis=0, tiled=True)
    label = lax.all_gather(label, "front", axis=0, tiled=True)
    wanted = (lax.axis_index("front") * row_tiles + jnp.arange(row_tiles)).astype(F32)
    spread = (label[:, None] == wanted[None, :]).astype(F32)
    rows_full = jnp.einsum("qj,qrs->jrs", spread, product, precision=HI)
    rows_full = rows_full.reshape(row_tiles * 128, width)
    extended = lax.psum_scatter(rows_full, ("row", "col"), scatter_dimension=0, tiled=True)
    sampled = direct + extended
    masked = jnp.where(jnp.arange(width)[None, :] < ranks[0, 0], sampled, 0.0)
    gram = lax.psum(jnp.dot(masked.T, masked, precision=HI), "col")
    gram = jnp.stack([gram[:half, :half], gram[half:, :half], gram[half:, half:]])
    return sampled, gram


def on_device(
    sizes, front_slab, samples, child_tiles, parent_front, parent_tile, column_tiles, ranks
):
    args = (samples, child_tiles, parent_front, parent_tile, column_tiles, ranks)
    if sizes["row"] == 4 and sizes["col"] == 2:
        sampled, gram = sampled_and_gram(sizes["front"], front_slab[0], *args)
    else:
        sampled, gram = sampled_and_gram_any(front_slab[0], *args)
    sampled, basis = leaf_bases(sampled, gram, ranks)
    return (sampled[None], basis[None])


def solution(mesh):
    in_specs = (
        P("front", "row", "col"),
        P(("row", "col"), None),
        P(("front", "row", "col"), None, None),
        P(("front", "row", "col"), None),
        P(("front", "row", "col")),
        P(("front", "row", "col"), None),
        P("front", "row"),
    )
    out_specs = (P("front", ("row", "col"), None), P("front", ("row", "col"), None))
    return jax.shard_map(
        functools.partial(on_device, dict(mesh.shape)),
        mesh=mesh,
        in_specs=in_specs,
        out_specs=out_specs,
        check_vma=False,
    )
```

time: 228 us -> 89.6 us (0.39)
  waiting for transfers between devices: 114 us -> 0 us
  Pallas kernels: 0 us -> 82.3 us
  other arithmetic: 59.9 us -> 0 us
  between operations: 16 us -> 1.3 us
  starting transfers between devices: 11.3 us -> 0 us
  matrix products: 11.2 us -> 0 us
  local copies, waits for them, and re-layouts: 15.7 us -> 5.7 us
    pallas_call x0 -> x2, Pallas kernels: none -> 82.3 us  [the longest x1 70.3 us: sampled_and_gram(): pl.pallas_call(functools.partial(sample_kernel, fronts), out_shape=(jax.S...]
    another operation x10 -> x0, other arithmetic: 53.8 us -> none  [the longest x6 34 us: on_device(): lower = jnp.linalg.cholesky(gram)]
    reduce_scatter x2 -> x0, waiting for transfers between devices: 38.5 us -> none  [the longest x1 38.5 us: on_device(): lax.psum_scatter(rows_full, ('row', 'col'), scatter_dimension=0, tiled=True)]
    all_gather x1 -> x0, waiting for transfers between devices: 30.4 us -> none  [on_device(): omega = lax.all_gather(samples, ('row', 'col'), axis=0, tiled=True)]
    psum x1 -> x0, waiting for transfers between devices: 22.9 us -> none  [on_device(): gram = lax.psum(partial_gram, 'col') + jnp.diag(1.0 - mask)]
    all_to_all x2 -> x0, waiting for transfers between devices: 21 us -> none  [the longest x1 21 us: on_device(): lax.all_to_all(sent, 'front', split_axis=0, concat_axis=0, tiled=True)]
    all_to_all x2 -> x0, starting transfers between devices: 10.9 us -> none  [the longest x1 6.35 us: on_device(): lax.all_to_all(labels, 'front', split_axis=0, concat_axis=0, tiled=True)]
    dot_general x6 -> x0, matrix products: 9.73 us -> none  [the longest x1 4.93 us: on_device(): jnp.dot(slab, own, preferred_element_type=jnp.float32)]
  transfers between devices with their start and end apart: 6 -> 0, of which waited for: 4 -> 0; matrix products, arithmetic and copies ran while one was open for 9% -> 0% of each run, Pallas kernels for 0% -> 0%
where the time goes in v1:
time: 89.6 us; the launch traced here: 89.3 us
  Pallas kernels  82.3 us (92%)
  local copies, waits for them, and re-layouts  5.7 us (6%)
  between operations  1.3 us (1%)
    pallas_call x1, Pallas kernels, sampled_and_gram(): pl.pallas_call(functools.partial(sample_kernel, fronts), out_shape=(jax.S...  70.3 us
    pallas_call x1, Pallas kernels, leaf_bases(): pl.pallas_call(basis_kernel, out_shape=(jax.ShapeDtypeStruct(sampled.shap...  12 us
    unnamed x13, local copies, waits for them, and re-layouts  5.7 us

profile of v1, /device:TPU:0, one launch (start us, length us, event | category | flops | bytes accessed | tf_op | source)
XLA Modules:
  0.0 89.3 jit_solution(8817917169618497055)
XLA Ops:
  1.3 0.7 copy.9.front_ref
  2.0 0.0 copy-start
  2.0 1.2 %copy-done = bf16[2,128,2048]{2,1,0:T(8,128)(2,1)S(1)} copy-done((bf16[2,128,2048]{2,1,0:T(8,128)(2,1)S(1)}, bf16[2,128,2048]{2,1,0:T(8,128)(2,1)}, u32[]{:S(2)}) %copy-start) | copy-done | bytes 1048600
  3.2 0.0 copy-start.1
  3.2 1.0 %copy-done.1 = bf16[1024,256]{1,0:T(8,128)(2,1)S(1)} copy-done((bf16[1024,256]{1,0:T(8,128)(2,1)S(1)}, bf16[1024,256]{1,0:T(8,128)(2,1)}, u32[]{:S(2)}) %copy-start.1) | copy-done | bytes 524312
  4.3 0.0 copy-start.4
  4.3 0.7 copy-done.4
  5.0 0.0 copy-start.5
  5.0 0.7 copy-done.5
  5.6 70.3 %sampled_and_gram.1 = (f32[256,256]{1,0:T(8,128)S(1)}, f32[3,128,128]{2,1,0:T(8,128)S(1)}) custom-call(s32[2]{0:T(128)S(1)} %copy-done.5, s32[2,1]{1,0:T(2,128)S(1)} %copy.9.front_ref, s32[2,16]{1,0:T(2,128)S(1)} %copy-done.4, s32[1,1]{1,0:T(1,128)S(6)} %copy.10.rank_ref, bf16[512,4096]{1,0:T(8,128)(2,1)} %bitcast.5, bf16[8,128,256]{2,1,0:T(8,128)(2,1)S(1)} %bitcast.4, ...), custom_call_target="tpu_custom_call" | custom-call | tf_op jit(solution)/shard_map/sampled_and_gram/pallas_call | solution.py:391
  75.9 0.0 copy-start.2
  75.9 0.7 copy-done.2
  76.6 0.0 copy-start.3
  76.6 0.7 copy-done.3
  77.3 12.0 %leaf_bases.1 = (f32[256,256]{1,0:T(8,128)}, f32[256,256]{1,0:T(8,128)}) custom-call(s32[1,1]{1,0:T(1,128)S(6)} %copy.10.rank_ref, f32[256,256]{1,0:T(8,128)} %copy-done.2, f32[3,128,128]{2,1,0:T(8,128)} %copy-done.3), custom_call_target="tpu_custom_call" | custom-call | tf_op jit(solution)/shard_map/leaf_bases/pallas_call | solution.py:79
Async XLA Ops:
  2.0 1.2 %copy-start = (bf16[2,128,2048]{2,1,0:T(8,128)(2,1)S(1)}, bf16[2,128,2048]{2,1,0:T(8,128)(2,1)}, u32[]{:S(2)}) copy-start(bf16[2,128,2048]{2,1,0:T(8,128)(2,1)} %child_ref.1) | copy-start | bytes 3145732
  3.2 1.0 %copy-start.1 = (bf16[1024,256]{1,0:T(8,128)(2,1)S(1)}, bf16[1024,256]{1,0:T(8,128)(2,1)}, u32[]{:S(2)}) copy-start(bf16[1024,256]{1,0:T(8,128)(2,1)} %param.8) | copy-start | bytes 1572868
  4.3 0.7 copy-start.4
  5.0 0.7 copy-start.5
  75.9 0.7 copy-start.2
  76.6 0.7 copy-start.3

commit v2 on v1

v2 whole, which is shorter than its diff:
```python
import functools

import jax
import jax.numpy as jnp
from jax import lax
from jax.experimental import pallas as pl
from jax.experimental.pallas import tpu as pltpu
from jax.sharding import PartitionSpec as P

F32 = jnp.float32
HI = lax.Precision.HIGHEST
LOGICAL = pl.DeviceIdType.MESH


def dot_nt(a, b):
    return lax.dot_general(a, b, (((1,), (1,)), ((), ())), precision=HI, preferred_element_type=F32)


def inverse_factor(a):
    n = a.shape[0]
    tiles = n // 8
    w = [a[8 * t : 8 * t + 8, :] for t in range(tiles)]
    lane = lax.broadcasted_iota(jnp.int32, (8, n), 1)
    sub = lax.broadcasted_iota(jnp.int32, (8, n), 0)
    rows = []
    for t in range(tiles):
        base = 8 * t
        inside = (lane >= base) & (lane < base + 8)
        cols = [jnp.broadcast_to(w[t][:, base + k : base + k + 1], (8, n)) for k in range(8)]
        v = jnp.where(inside, jnp.where(lane - base == sub, 1.0, 0.0), w[t])
        done, pivots = v, cols[0]
        for k in range(8):
            here = sub == k
            pivot = jnp.broadcast_to(cols[k][k : k + 1, :], (8, n))
            inv = 1.0 / pivot
            done = jnp.where(here, v, done)
            pivots = jnp.where(here, pivot, pivots)
            step = jnp.broadcast_to(v[k : k + 1, :], (8, n)) * inv
            v = jnp.where(here, step, v - cols[k] * step)
            for m in range(k + 1, 8):
                step = jnp.broadcast_to(cols[m][k : k + 1, :], (8, n)) * inv
                cols[m] = jnp.where(here, step, cols[m] - cols[k] * step)
        rows.append(jnp.where(lane < base + 8, done, 0.0) * lax.rsqrt(pivots))
        vk = [jnp.broadcast_to(v[k : k + 1, :], (8, n)) for k in range(8)]
        for u in range(t + 1, tiles):
            x = jnp.where(inside, 0.0, w[u])
            terms = [
                jnp.broadcast_to(w[u][:, base + k : base + k + 1], (8, n)) * vk[k] for k in range(8)
            ]
            low = (terms[0] + terms[1]) + (terms[2] + terms[3])
            high = (terms[4] + terms[5]) + (terms[6] + terms[7])
            w[u] = x - (low + high)
    return jnp.concatenate(rows, axis=0)


def basis_kernel(sampled_ref, gram_ref, out_ref, basis_ref):
    half = gram_ref.shape[2]
    rank = gram_ref[0, half : half + 1, :]
    sampled = sampled_ref[...]
    out_ref[...] = sampled
    rows = sampled.shape[0]
    lane = lax.broadcasted_iota(jnp.int32, (rows, half), 1).astype(F32)
    first = jnp.where(lane < rank, sampled[:, :half], 0.0)
    second = jnp.where(lane + half < rank, sampled[:, half:], 0.0)
    r = lax.broadcasted_iota(jnp.int32, (half, half), 0)
    c = lax.broadcasted_iota(jnp.int32, (half, half), 1)
    lane = c.astype(F32)
    a = gram_ref[0, :half, :] + jnp.where((r == c) & (lane >= rank), 1.0, 0.0)
    inv1 = inverse_factor(a)
    low = dot_nt(gram_ref[1, :half, :], inv1)
    a = gram_ref[2, :half, :] + jnp.where((r == c) & (lane + half >= rank), 1.0, 0.0)
    a = a - dot_nt(low, low)
    inv2 = inverse_factor(a)
    basis = dot_nt(first, inv1)
    basis_ref[:, :half] = basis
    basis_ref[:, half:] = dot_nt(second - dot_nt(basis, low), inv2)


def leaf_bases(sampled, gram):
    vmem = pl.BlockSpec(memory_space=pltpu.VMEM)
    return pl.pallas_call(
        basis_kernel,
        out_shape=(jax.ShapeDtypeStruct(sampled.shape, F32),) * 2,
        in_specs=[vmem, vmem],
        out_specs=(vmem, vmem),
        name="leaf_bases",
    )(sampled, gram)


def sample_kernel(
    fronts,
    tile_hbm,
    front_hbm,
    column_hbm,
    rank_hbm,
    slab_ref,
    samples_ref,
    child_ref,
    sampled_ref,
    gram_ref,
    tile_ref,
    front_ref,
    column_ref,
    rank_ref,
    omega,
    slab,
    child,
    held,
    part,
    blocks,
    got1,
    got2,
    gram_own,
    gram_got,
    copy_sem,
    gs,
    gr,
    zs_right,
    zs_left,
    zs_pair,
    zr,
    zr_pair,
    es,
    er,
):
    f, r, c = lax.axis_index("front"), lax.axis_index("row"), lax.axis_index("col")
    x, core = r // 2, r % 2
    width = samples_ref.shape[2]
    half = width // 2
    chunk = samples_ref.shape[0]
    piece = chunk // 4
    odd = f % 2
    count = child_ref.shape[0]
    slab_rows, slab_cols = slab_ref.shape
    own_rows = slab_rows // 2
    pieces = own_rows // 128
    row_tiles = slab_rows * 4 // 128
    r_x = (1 - x) * 2 + core
    r_p = x * 2 + (1 - core)
    to_x, to_y, to_p = (f, r_x, c), (f, r, 1 - c), (f, r_p, c)
    right, left = (f + 1, r, c), (f - 1, r, c)

    loads = [
        pltpu.make_async_copy(child_ref, child, copy_sem.at[0]),
        pltpu.make_async_copy(slab_ref, slab, copy_sem.at[1]),
        pltpu.make_async_copy(
            samples_ref, omega.at[pl.ds((r * 2 + c) * chunk, chunk)], copy_sem.at[2]
        ),
    ]
    small = [
        pltpu.make_async_copy(src, dst, copy_sem.at[3 + n])
        for n, (src, dst) in enumerate(
            (
                (tile_hbm, tile_ref),
                (front_hbm, front_ref),
                (column_hbm, column_ref),
                (rank_hbm, rank_ref),
            )
        )
    ]
    loads[2].start()
    for cp in small:
        cp.start()
    loads[0].start()
    loads[1].start()

    barrier = pltpu.get_barrier_semaphore()
    for target in (to_x, to_y, to_p):
        pl.semaphore_signal(barrier, inc=1, device_id=target, device_id_type=LOGICAL)

    @pl.when(f < fronts - 1)
    def _():
        pl.semaphore_signal(barrier, inc=1, device_id=right, device_id_type=LOGICAL)

    @pl.when(f > 0)
    def _():
        pl.semaphore_signal(barrier, inc=1, device_id=left, device_id_type=LOGICAL)

    pl.semaphore_wait(barrier, 3 + jnp.minimum(f, 1) + jnp.minimum(fronts - 1 - f, 1))

    def rcopy(src, dst, send, recv, target):
        return pltpu.make_async_remote_copy(
            src_ref=src,
            dst_ref=dst,
            send_sem=send,
            recv_sem=recv,
            device_id=target,
            device_id_type=LOGICAL,
        )

    to_z = (f + 1 - 2 * odd, r, c)

    def where_is(row, col, i):
        q = i + odd * (3 - 2 * i)
        return pl.ds((row * 2 + col) * chunk + q * piece, piece)

    sent = []

    def send(place, n, target, src=None):
        src = omega.at[place] if src is None else src
        cp = rcopy(src, omega.at[place], gs.at[n], gr.at[n], target)
        cp.start()
        sent.append(cp)

    def arrived(place, n):
        rcopy(omega.at[place], omega.at[place], gs.at[n], gr.at[n], to_p).wait_recv()

    def own(i):
        return samples_ref.at[pl.ds((i + odd * (3 - 2 * i)) * piece, piece)]

    for i, j in ((0, 1), (1, 0), (2, 2)):
        send(where_is(r, c, i), i, to_x, own(i))
        send(where_is(r, c, j), 3 + j, to_y, own(j))
    for i in range(4):
        send(where_is(r, c, i), 12 + i, to_p, own(i))
    x_at = functools.partial(where_is, r_x, c)
    y_at = functools.partial(where_is, r, 1 - c)
    d_at = functools.partial(where_is, r_x, 1 - c)
    arrived(x_at(0), 0)
    send(x_at(0), 6, to_y)
    send(x_at(0), 8, to_z)
    arrived(y_at(1), 4)
    send(y_at(1), 7, to_x)
    send(x_at(0), 16, to_p)
    send(y_at(1), 21, to_p)
    arrived(y_at(0), 3)
    send(y_at(0), 9, to_z)
    send(y_at(0), 20, to_p)
    arrived(x_at(1), 1)
    send(x_at(1), 17, to_p)
    arrived(x_at(3), 8)
    send(x_at(3), 19, to_p)
    arrived(d_at(0), 6)
    send(d_at(0), 10, to_z)
    send(d_at(0), 24, to_p)
    arrived(d_at(1), 7)
    send(d_at(1), 11, to_z)
    send(d_at(1), 25, to_p)
    arrived(y_at(3), 9)
    send(y_at(3), 23, to_p)
    arrived(x_at(2), 2)
    send(x_at(2), 18, to_p)
    arrived(y_at(2), 5)
    send(y_at(2), 22, to_p)
    arrived(d_at(3), 10)
    send(d_at(3), 27, to_p)
    arrived(d_at(2), 11)
    send(d_at(2), 26, to_p)
    r_d = r_x + r_p - r
    for i in range(4):
        arrived(where_is(r_p, c, i), 12 + i)
        arrived(where_is(r_d, c, i), 16 + i)
        arrived(where_is(r_p, 1 - c, i), 20 + i)
        arrived(where_is(r_d, 1 - c, i), 24 + i)
    for cp in small:
        cp.wait()
    loads[2].wait()
    loads[0].wait()

    def tile_row(p, t):
        return 8 + 64 * (p * count + t)

    group = 2
    labels = jnp.zeros((8, width), F32)
    for t in range(count):
        acc = jnp.zeros((128, width), F32)
        for b in range(0, column_ref.shape[1], group):
            chosen = jnp.concatenate(
                [
                    omega[column_ref[t, b + g]]
                    for g in range(group)
                ],
                axis=0,
            )
            acc = acc + jnp.dot(
                child[t, :, 128 * b : 128 * (b + group)], chosen, preferred_element_type=F32
            )
        for p in range(2):
            at = tile_row(p, t)
            held[0, f, at : at + 64, :] = acc[64 * p : 64 * (p + 1)]
        label = (front_ref[t, 0] * row_tiles + tile_ref[t]).astype(F32)
        labels = jnp.where(lax.broadcasted_iota(jnp.int32, (8, width), 0) == t, label, labels)
    held[0, f, 0:8, :] = labels

    spans = [pl.ds(0, tile_row(1, 0)), pl.ds(tile_row(1, 0), 64 * count)]

    def along(src, p, sem, target):
        ref = held.at[0, src, spans[p]]
        return rcopy(ref, ref, sem.at[p, src], zr.at[p, src], target)

    def across(src, p):
        return rcopy(
            held.at[0, src, spans[p]],
            held.at[1, src, spans[p]],
            zs_pair.at[p, src],
            zr_pair.at[p, src],
            to_p,
        )

    for p in range(2):

        @pl.when(f < fronts - 1)
        def _():
            along(f, p, zs_right, right).start()

        @pl.when(f > 0)
        def _():
            along(f, p, zs_left, left).start()

        across(f, p).start()

    loads[1].wait()

    @pl.loop(0, slab_rows // 128)
    def _(i):
        rows = pl.ds(pl.multiple_of(i * 128, 128), 128)
        part[rows, :] = jnp.dot(
            slab[rows, :],
            omega[pl.ds(c * (slab_cols // 128), slab_cols // 128)].reshape(slab_cols, width),
            preferred_element_type=F32,
        )

    def relay(p):
        for d in range(1, fronts):

            @pl.when(f >= d)
            def _():
                along(f - d, p, zs_right, right).wait_recv()

                @pl.when(f < fronts - 1)
                def _():
                    along(f - d, p, zs_right, right).start()

                across(f - d, p).start()

            @pl.when(f + d < fronts)
            def _():
                along(f + d, p, zs_left, left).wait_recv()

                @pl.when(f > 0)
                def _():
                    along(f + d, p, zs_left, left).start()

                across(f + d, p).start()

        for s in range(fronts):
            across(s, p).wait_recv()

    def fill(p, h, spot, row, col, piece_of_part):
        lanes = slice(h * half, (h + 1) * half)
        first = f * row_tiles + (row * 2 + col) * pieces
        for i in range(pieces):
            wanted = (first + i).astype(F32)
            masks = []
            for side in range(2):
                for s in range(fronts):
                    for t in range(count):
                        label = jnp.broadcast_to(held[side, s, t : t + 1, :half], (8, half))
                        masks.append((side, s, t, label == wanted))

            @pl.loop(0, 2)
            def _(q):
                accs = [jnp.zeros((8, half), F32)] * 4
                if piece_of_part is not None:
                    at = piece_of_part * own_rows + i * 128 + p * 64 + q * 32
                    accs = [part[pl.ds(pl.multiple_of(at + 8 * e, 8), 8), lanes] for e in range(4)]
                for side, s, t, mask in masks:
                    for e in range(4):
                        rows = pl.ds(pl.multiple_of(tile_row(p, t) + q * 32 + 8 * e, 8), 8)
                        accs[e] = accs[e] + jnp.where(mask, held[side, s, rows, lanes], 0.0)
                for e in range(4):
                    rows = pl.ds(pl.multiple_of(i * 64 + q * 32 + 8 * e, 8), 8)
                    blocks[p, h, spot, rows, :] = accs[e]

    two = pl.ds(2, 2)
    first_hop = [
        [
            rcopy(blocks.at[p, h, two], got1.at[p, h], es.at[p, h], er.at[p, h], to)
            for h, to in ((0, to_x), (1, to_y))
        ]
        for p in range(2)
    ]
    second_hop = [
        [
            rcopy(blocks.at[p, h, 1], got2.at[p, h], es.at[p, 2 + h], er.at[p, 2 + h], to)
            for h, to in ((0, to_y), (1, to_x))
        ]
        for p in range(2)
    ]

    def spread(p):
        fill(p, 0, 2, r_x, c, None)
        fill(p, 0, 3, r_x, 1 - c, None)
        first_hop[p][0].start()
        fill(p, 1, 2, r, 1 - c, 1 - c)
        fill(p, 1, 3, r_x, 1 - c, None)
        first_hop[p][1].start()
        fill(p, 0, 1, r, 1 - c, 1 - c)
        fill(p, 1, 1, r_x, c, None)
        fill(p, 0, 0, r, c, c)
        fill(p, 1, 0, r, c, c)

    def forward(p):
        for h in range(2):
            first_hop[p][h].wait_recv()
            blocks[p, h, 1] = blocks[p, h, 1] + got1[p, h, 1]
            second_hop[p][h].start()

    def finish(p):
        for h in range(2):
            second_hop[p][h].wait_recv()
            total = (blocks[p, h, 0] + got1[p, h, 0]) + got2[p, h]
            for i in range(pieces):
                at = i * 128 + p * 64
                sampled_ref[at : at + 64, h * half : (h + 1) * half] = total[64 * i : 64 * (i + 1)]

    relay(0)
    spread(0)
    relay(1)
    forward(0)
    spread(1)
    finish(0)
    forward(1)
    finish(1)
    lane = lax.broadcasted_iota(jnp.int32, (own_rows, half), 1)
    masked = []
    for h in range(2):
        total = sampled_ref[:, h * half : (h + 1) * half]
        masked.append(jnp.where(lane + h * half < rank_ref[0, 0], total, 0.0))
    for n, (i, j) in enumerate(((0, 0), (1, 0), (1, 1))):
        gram_own[n] = lax.dot_general(
            masked[i],
            masked[j],
            (((0,), (0,)), ((), ())),
            precision=HI,
            preferred_element_type=F32,
        )
    g = rcopy(gram_own, gram_got, es.at[0, 4], er.at[0, 4], to_y)
    g.start()
    for cp in sent:
        cp.wait_send()
    for p in range(2):
        for s in range(fronts):
            across(s, p).wait_send()

            @pl.when((f < fronts - 1) & (f >= s))
            def _():
                along(s, p, zs_right, right).wait_send()

            @pl.when((f > 0) & (f <= s))
            def _():
                along(s, p, zs_left, left).wait_send()

        for cp in first_hop[p] + second_hop[p]:
            cp.wait_send()
    g.wait()
    rank = jnp.full((3, 8, half), rank_ref[0, 0].astype(F32), F32)
    gram_ref[:, half : half + 8, :] = rank
    gram_ref[:, :half, :] = gram_own[...] + gram_got[...]


def sampled_and_gram(
    fronts, slab, samples, child_tiles, parent_front, parent_tile, column_tiles, ranks
):
    width = samples.shape[1]
    half = width // 2
    count = child_tiles.shape[0]
    rows = slab.shape[0] // 2
    hbm = pl.BlockSpec(memory_space=pl.ANY)
    vmem = pl.BlockSpec(memory_space=pltpu.VMEM)
    dma = lambda *n: pltpu.SemaphoreType.DMA(n)
    return pl.pallas_call(
        functools.partial(sample_kernel, fronts),
        out_shape=(
            jax.ShapeDtypeStruct((rows, width), F32),
            jax.ShapeDtypeStruct((3, half + 8, half), F32),
        ),
        in_specs=[hbm] * 7,
        out_specs=(vmem, vmem),
        scratch_shapes=[
            pltpu.SMEM(parent_tile.shape, jnp.int32),
            pltpu.SMEM(parent_front.shape, jnp.int32),
            pltpu.SMEM(column_tiles.shape, jnp.int32),
            pltpu.SMEM(ranks.shape, jnp.int32),
            pltpu.VMEM((samples.shape[0] // 128 * 8, 128, width), samples.dtype),
            pltpu.VMEM(slab.shape, slab.dtype),
            pltpu.VMEM(child_tiles.shape, child_tiles.dtype),
            pltpu.VMEM((2, fronts, 128 * count + 8, width), F32),
            pltpu.VMEM((slab.shape[0], width), F32),
            pltpu.VMEM((2, 2, 4, rows // 2, half), F32),
            pltpu.VMEM((2, 2, 2, rows // 2, half), F32),
            pltpu.VMEM((2, 2, rows // 2, half), F32),
            pltpu.VMEM((3, half, half), F32),
            pltpu.VMEM((3, half, half), F32),
            dma(7),
            dma(28),
            dma(28),
            dma(2, fronts),
            dma(2, fronts),
            dma(2, fronts),
            dma(2, fronts),
            dma(2, fronts),
            dma(2, 5),
            dma(2, 5),
        ],
        compiler_params=pltpu.CompilerParams(
            collective_id=0, has_side_effects=True, vmem_limit_bytes=67043328
        ),
        name="sampled_and_gram",
    )(
        parent_tile,
        parent_front,
        column_tiles,
        ranks,
        slab,
        samples.reshape(-1, 128, width),
        child_tiles,
    )


def sampled_and_gram_any(
    slab, samples, child_tiles, parent_front, parent_tile, column_tiles, ranks
):
    width = samples.shape[1]
    half = width // 2
    col_width = slab.shape[1]
    omega = lax.all_gather(samples, ("row", "col"), axis=0, tiled=True)
    own = lax.dynamic_slice_in_dim(omega, lax.axis_index("col") * col_width, col_width, 0)
    direct = lax.psum_scatter(
        jnp.dot(slab, own, preferred_element_type=F32), "col", scatter_dimension=0, tiled=True
    )
    count = child_tiles.shape[0]
    blocks = child_tiles.shape[2] // 128
    chosen = omega.reshape(-1, 128, width)[column_tiles]
    pieces = child_tiles.reshape(count, 128, blocks, 128)
    product = jnp.einsum("trkc,tkcs->trs", pieces, chosen, preferred_element_type=F32)
    row_tiles = slab.shape[0] * lax.axis_size("row") // 128
    label = (parent_front[:, 0] * row_tiles + parent_tile).astype(F32)
    product = lax.all_gather(product, "front", axis=0, tiled=True)
    label = lax.all_gather(label, "front", axis=0, tiled=True)
    wanted = (lax.axis_index("front") * row_tiles + jnp.arange(row_tiles)).astype(F32)
    spread = (label[:, None] == wanted[None, :]).astype(F32)
    rows_full = jnp.einsum("qj,qrs->jrs", spread, product, precision=HI)
    rows_full = rows_full.reshape(row_tiles * 128, width)
    extended = lax.psum_scatter(rows_full, ("row", "col"), scatter_dimension=0, tiled=True)
    sampled = direct + extended
    masked = jnp.where(jnp.arange(width)[None, :] < ranks[0, 0], sampled, 0.0)
    gram = lax.psum(jnp.dot(masked.T, masked, precision=HI), "col")
    gram = jnp.stack([gram[:half, :half], gram[half:, :half], gram[half:, half:]])
    rank = jnp.broadcast_to(ranks.astype(F32)[:, :, None], (3, 8, half))
    return sampled, jnp.concatenate([gram, rank], axis=1)


def on_device(
    sizes, front_slab, samples, child_tiles, parent_front, parent_tile, column_tiles, ranks
):
    args = (samples, child_tiles, parent_front, parent_tile, column_tiles, ranks)
    if sizes["row"] == 4 and sizes["col"] == 2 and sizes["front"] % 2 == 0:
        sampled, gram = sampled_and_gram(sizes["front"], front_slab[0], *args)
    else:
        sampled, gram = sampled_and_gram_any(front_slab[0], *args)
    sampled, basis = leaf_bases(sampled, gram)
    return (sampled[None], basis[None])


def solution(mesh):
    in_specs = (
        P("front", "row", "col"),
        P(("row", "col"), None),
        P(("front", "row", "col"), None, None),
        P(("front", "row", "col"), None),
        P(("front", "row", "col")),
        P(("front", "row", "col"), None),
        P("front", "row"),
    )
    out_specs = (P("front", ("row", "col"), None), P("front", ("row", "col"), None))
    return jax.shard_map(
        functools.partial(on_device, dict(mesh.shape)),
        mesh=mesh,
        in_specs=in_specs,
        out_specs=out_specs,
        check_vma=False,
    )
```

time: 89.6 us -> 80.3 us (0.90)
  Pallas kernels: 82.3 us -> 77.6 us
  local copies, waits for them, and re-layouts: 5.7 us -> 1.3 us
    pallas_call x1, Pallas kernels: 70.3 us -> 65.5 us  [sampled_and_gram(): pl.pallas_call(functools.partial(sample_kernel, fronts), out_shape=(jax.S...]
    unnamed x13 -> x1, local copies, waits for them, and re-layouts: 5.7 us -> 1.3 us
where the time goes in v2:
time: 80.3 us; the launch traced here: 80.2 us
  Pallas kernels  77.6 us (97%)
  local copies, waits for them, and re-layouts  1.3 us (2%)
  between operations  1.29 us (2%)
    pallas_call x1, Pallas kernels, sampled_and_gram(): pl.pallas_call(functools.partial(sample_kernel, fronts), out_shape=(jax.S...  65.5 us
    pallas_call x1, Pallas kernels, leaf_bases(): pl.pallas_call(basis_kernel, out_shape=(jax.ShapeDtypeStruct(sampled.shap...  12 us

profile of v2, /device:TPU:0, one launch (start us, length us, event | category | flops | bytes accessed | tf_op | source)
XLA Modules:
  0.0 80.2 jit_solution(1434740471251603295)
XLA Ops:
  1.3 1.3 %copy.9.front_hbm = s32[2,1]{1,0:T(2,128)} copy(s32[2,1]{0,1:T(1,128)} %param.10) | data formatting | bytes 16 | tf_op args[3]
  2.6 65.5 %sampled_and_gram.1 = (f32[256,256]{1,0:T(8,128)}, f32[3,136,128]{2,1,0:T(8,128)}) custom-call(s32[2]{0:T(128)} %tile_hbm.1, s32[2,1]{1,0:T(2,128)} %copy.9.front_hbm, s32[2,16]{1,0:T(2,128)} %column_hbm.1, s32[1,1]{1,0:T(1,128)S(6)} %copy.10.rank_hbm, bf16[512,4096]{1,0:T(8,128)(2,1)} %bitcast.4, bf16[8,128,256]{2,1,0:T(8,128)(2,1)} %bitcast.5, ...), custom_call_target="tpu_custom_call" | custom-call | tf_op jit(solution)/shard_map/sampled_and_gram/pallas_call | solution.py:472
  68.1 12.0 %leaf_bases.1 = (f32[256,256]{1,0:T(8,128)}, f32[256,256]{1,0:T(8,128)}) custom-call(f32[256,256]{1,0:T(8,128)} %get-tuple-element.6.sampled_ref, f32[3,136,128]{2,1,0:T(8,128)} %get-tuple-element.7.gram_ref), custom_call_target="tpu_custom_call" | custom-call | tf_op jit(solution)/shard_map/leaf_bases/pallas_call | solution.py:81
